TPU v7x, 32 devices: a whole 2x2x4 slice. The times are simulated.
32 devices in a mesh: row: 4 (over x, core), col: 8 (over z, y).
Axes of the slice: x: 2, y: 2, z: 4, core: 2. Of those that a mesh axis runs over, the one named last changes fastest.
Arguments:
- features: bfloat16 [8192, 256], P(('col', 'row')), may hold values from -6 to 6
- weight: bfloat16 [256, 256], replicated, may hold values from -0.375 to 0.375
- grad_out: bfloat16 [8192, 256], P(('row', 'col')), may hold values from -6 to 6
- adj_values: bfloat16 [384, 1024, 128], P('row', 'col'), may hold values from -0.15625 to 0.15625
- block_pos: int32 [4, 768], P('row', 'col'), may hold values from 0 to 127, as said below
- block_count: int32 [4, 8], P('row', 'col'), may hold values from 24 to 96, as said below
Outputs:
- activation: bfloat16 [8192, 256], P(('row', 'col'))
- grad_input: bfloat16 [8192, 256], P(('col', 'row'))
- grad_weight: float32 [256, 256], replicated
Inputs may be any that keep to these rules, and one draw needn't show every extreme that they name: `block_pos`: within one tile the block positions of all 96 slots are distinct values below 128. `block_count`: some tile has exactly 96 live slots and some tile exactly 24.
All inputs are finite; a program needn't handle non-finite values.
Results may differ from a plain program's by a relative error of at most 0.018.
Values may be sent and summed in bfloat16 or wider, within the bound.
A program may use at most 128 MiB of HBM per device.

v0:
```python
import jax
import jax.numpy as jnp
from jax import lax
from jax.sharding import PartitionSpec as P


def tile_forward(values, positions, live_count, panel, row_blocks, col_blocks):
    slots = values.shape[0]
    block_size = values.shape[1]
    width = panel.shape[1]
    groups = 6
    per_group = slots // groups
    brow = positions // col_blocks
    bcol = positions % col_blocks
    live = (jnp.arange(slots, dtype=jnp.int32) < live_count).astype(jnp.float32)
    blocks = panel.reshape(col_blocks, block_size, width)

    def step(totals, items):
        vals, rows_idx, cols_idx, alive = items
        picked = blocks[cols_idx]
        prod = jnp.einsum("kij,kjf->kif", vals, picked, preferred_element_type=jnp.float32)
        onehot = (rows_idx[None, :] == jnp.arange(row_blocks, dtype=jnp.int32)[:, None]).astype(
            jnp.float32
        ) * alive[None, :]
        return (totals + jnp.einsum("bk,kif->bif", onehot, prod), None)

    items = (
        values.reshape(groups, per_group, block_size, block_size),
        brow.reshape(groups, per_group),
        bcol.reshape(groups, per_group),
        live.reshape(groups, per_group),
    )
    start = jnp.zeros((row_blocks, block_size, width), jnp.float32)
    totals, unused = lax.scan(step, start, items)
    return totals.reshape(row_blocks * block_size, width)


def tile_backward(values, positions, live_count, grads, row_blocks, col_blocks):
    slots = values.shape[0]
    block_size = values.shape[1]
    width = grads.shape[1]
    groups = 6
    per_group = slots // groups
    brow = positions // col_blocks
    bcol = positions % col_blocks
    live = (jnp.arange(slots, dtype=jnp.int32) < live_count).astype(jnp.float32)
    blocks = grads.reshape(row_blocks, block_size, width)

    def step(totals, items):
        vals, rows_idx, cols_idx, alive = items
        picked = blocks[rows_idx]
        prod = jnp.einsum("kij,kif->kjf", vals, picked, preferred_element_type=jnp.float32)
        onehot = (cols_idx[None, :] == jnp.arange(col_blocks, dtype=jnp.int32)[:, None]).astype(
            jnp.float32
        ) * alive[None, :]
        return (totals + jnp.einsum("bk,kjf->bjf", onehot, prod), None)

    items = (
        values.reshape(groups, per_group, block_size, block_size),
        brow.reshape(groups, per_group),
        bcol.reshape(groups, per_group),
        live.reshape(groups, per_group),
    )
    start = jnp.zeros((col_blocks, block_size, width), jnp.float32)
    totals, unused = lax.scan(step, start, items)
    return totals.reshape(col_blocks * block_size, width)


def body(features, weight, grad_out, adj_values, block_pos, block_count):
    block_size = adj_values.shape[2]
    rows_tile = grad_out.shape[0] * lax.axis_size("col")
    row_blocks = rows_tile // block_size
    projected = jnp.dot(features, weight, preferred_element_type=jnp.float32).astype(jnp.bfloat16)
    panel = lax.all_gather(projected, "row", axis=0, tiled=True)
    col_blocks = panel.shape[0] // block_size
    positions = block_pos[0]
    live_count = block_count[0, 0]
    partial_value = tile_forward(adj_values, positions, live_count, panel, row_blocks, col_blocks)
    hidden = lax.psum_scatter(
        partial_value.astype(jnp.bfloat16), "col", scatter_dimension=0, tiled=True
    ).astype(jnp.float32)
    sigma = jax.nn.sigmoid(hidden)
    activation = (hidden * sigma).astype(jnp.bfloat16)
    grad_hidden = (grad_out.astype(jnp.float32) * sigma * (1.0 + hidden * (1.0 - sigma))).astype(
        jnp.bfloat16
    )
    grad_panel = lax.all_gather(grad_hidden, "col", axis=0, tiled=True)
    partial_back = tile_backward(
        adj_values, positions, live_count, grad_panel, row_blocks, col_blocks
    )
    grad_xw = lax.psum_scatter(
        partial_back.astype(jnp.bfloat16), "row", scatter_dimension=0, tiled=True
    )
    local_weight = lax.dot_general(
        features, grad_xw, (((0,), (0,)), ((), ())), preferred_element_type=jnp.float32
    )
    grad_weight = lax.psum(local_weight, ("row", "col"))
    grad_input = lax.dot_general(
        grad_xw, weight, (((1,), (1,)), ((), ())), preferred_element_type=jnp.float32
    ).astype(jnp.bfloat16)
    return (activation, grad_input, grad_weight)


def solution(mesh):
    placed = (
        P(("col", "row"), None),
        P(),
        P(("row", "col"), None),
        P("row", "col", None),
        P("row", "col"),
        P("row", "col"),
    )
    return jax.shard_map(
        body,
        mesh=mesh,
        in_specs=placed,
        out_specs=(P(("row", "col"), None), P(("col", "row"), None), P()),
        check_vma=False,
    )
```

profile of v0, /device:TPU:0, one launch (start us, length us, event | category | flops | bytes accessed | tf_op | source)
XLA Modules:
  0.0 351.3 jit_solution(11104023459522061868)
XLA Ops:
  7.7 1.3 reduce.3
  9.8 1.1 convolution_convert_fusion.1
  10.9 8.6 %all_gather.6 = bf16[1024,256]{1,0:T(8,128)(2,1)S(1)} all-gather(bf16[256,256]{1,0:T(8,128)(2,1)S(1)} %convolution_convert_fusion.1), channel_id=1, replica_groups=mesh['row'=4,'col'=8] {'row'}, dimensions={0}, use_global_device_ids=true | all-gather | bytes 655360 | tf_op jit(solution)/shard_map/all_gather | solution.py:74
  19.6 33.6 %while.22 = (s32[]{:T(128)}, f32[16,128,256]{2,0,1:T(8,128)}, s32[6,16]{1,0:T(8,128)S(1)}, bf16[6,16]{1,0:T(8,128)(2,1)S(1)}, bf16[6,16,128,128]{3,2,1,0:T(8,128...) while((s32[]{:T(128)}, f32[16,128,256]{2,0,1:T(8,128)}, ...), condition=%wide.region_1.2_spmd.clone, body=%wide.region_0.1_spmd.clone.sunk | while | flops 152045104 | bytes 9966739 | solution.py:34
  19.6 0.6 gather_fusion
  20.2 1.5 fusion.77
  21.7 2.1 select_add_fusion.2
  24.5 1.5 fusion.77
  26.0 3.7 %select_add_fusion.2 = f32[16,128,256]{2,0,1:T(8,128)} fusion(f32[16,128,256]{2,0,1:T(8,128)} %get-tuple-element.261, bf16[16,128,256]{2,1,0:T(8,128)(2,1)S(1)} %fusion.77, pred[]{:T(512)S(6)} %compare.11, bf16[16]{0:T(256)(128)(2,1)S(1)} %fusion.78, s32[16]{0:T(128)S(1)} %fusion.79), kind=kOutput, calls=%fused_computation.4.clone.1 | convolution fusion | flops 17826304 | bytes 5242977 | tf_op jit(solution)/shard_map/while/body/eval_jaxpr/bk,kif->bif/dot_general | solution.py:25
  30.4 1.5 fusion.77
  31.9 3.7 %select_add_fusion.2 = f32[16,128,256]{2,0,1:T(8,128)} fusion(f32[16,128,256]{2,0,1:T(8,128)} %get-tuple-element.261, bf16[16,128,256]{2,1,0:T(8,128)(2,1)S(1)} %fusion.77, pred[]{:T(512)S(6)} %compare.11, bf16[16]{0:T(256)(128)(2,1)S(1)} %fusion.78, s32[16]{0:T(128)S(1)} %fusion.79), kind=kOutput, calls=%fused_computation.4.clone.1 | convolution fusion | flops 17826304 | bytes 5242977 | tf_op jit(solution)/shard_map/while/body/eval_jaxpr/bk,kif->bif/dot_general | solution.py:25
  35.6 0.6 gather_fusion
  36.2 1.5 fusion.77
  37.7 3.7 %select_add_fusion.2 = f32[16,128,256]{2,0,1:T(8,128)} fusion(f32[16,128,256]{2,0,1:T(8,128)} %get-tuple-element.261, bf16[16,128,256]{2,1,0:T(8,128)(2,1)S(1)} %fusion.77, pred[]{:T(512)S(6)} %compare.11, bf16[16]{0:T(256)(128)(2,1)S(1)} %fusion.78, s32[16]{0:T(128)S(1)} %fusion.79), kind=kOutput, calls=%fused_computation.4.clone.1 | convolution fusion | flops 17826304 | bytes 5242977 | tf_op jit(solution)/shard_map/while/body/eval_jaxpr/bk,kif->bif/dot_general | solution.py:25
  42.1 1.5 fusion.77
  43.6 3.7 %select_add_fusion.2 = f32[16,128,256]{2,0,1:T(8,128)} fusion(f32[16,128,256]{2,0,1:T(8,128)} %get-tuple-element.261, bf16[16,128,256]{2,1,0:T(8,128)(2,1)S(1)} %fusion.77, pred[]{:T(512)S(6)} %compare.11, bf16[16]{0:T(256)(128)(2,1)S(1)} %fusion.78, s32[16]{0:T(128)S(1)} %fusion.79), kind=kOutput, calls=%fused_computation.4.clone.1 | convolution fusion | flops 17826304 | bytes 5242977 | tf_op jit(solution)/shard_map/while/body/eval_jaxpr/bk,kif->bif/dot_general | solution.py:25
  48.0 1.5 fusion.77
  49.5 3.7 %select_add_fusion.2 = f32[16,128,256]{2,0,1:T(8,128)} fusion(f32[16,128,256]{2,0,1:T(8,128)} %get-tuple-element.261, bf16[16,128,256]{2,1,0:T(8,128)(2,1)S(1)} %fusion.77, pred[]{:T(512)S(6)} %compare.11, bf16[16]{0:T(256)(128)(2,1)S(1)} %fusion.78, s32[16]{0:T(128)S(1)} %fusion.79), kind=kOutput, calls=%fused_computation.4.clone.1 | convolution fusion | flops 17826304 | bytes 5242977 | tf_op jit(solution)/shard_map/while/body/eval_jaxpr/bk,kif->bif/dot_general | solution.py:25
  53.2 1.7 convert_element_type.39
  55.0 1.3 copy.11
  56.4 65.1 %reduce-scatter.3.cloned.1.call-done = bf16[256,256]{1,0:T(8,128)(2,1)} async-done(((bf16[2048,256]{1,0:T(8,128)(2,1)}), bf16[256,256]{1,0:T(8,128)(2,1)}) %reduce-scatter.3.cloned.1.call-update) | async-done | bytes 131088 | tf_op jit(solution)/shard_map/reduce_scatter | solution.py:79
  121.5 1.7 fusion.43
  123.3 40.2 %all-gather.2.cloned.1.call-done = bf16[2048,256]{1,0:T(8,128)(2,1)} async-done(((bf16[256,256]{1,0:T(8,128)(2,1)}), bf16[2048,256]{1,0:T(8,128)(2,1)}) %all-gather.2.cloned.1.call-update) | async-done | bytes 1048592 | tf_op jit(solution)/shard_map/all_gather | solution.py:87
  163.5 25.3 %while.23 = (s32[]{:T(128)}, f32[8,128,256]{2,0,1:T(8,128)S(1)}, s32[6,16]{1,0:T(8,128)S(1)}, bf16[6,16]{1,0:T(8,128)(2,1)S(1)}, bf16[6,16,128,128]{3,2,1,0:T(8,...) while((s32[]{:T(128)}, f32[8,128,256]{2,0,1:T(8,128)S(1)}, ...), condition=%wide.region_4.5_spmd.clone, body=%wide.region_3.4_spmd.clone.sunk | while | flops 143131952 | bytes 7869587 | solution.py:65
  163.5 1.8 gather_fusion.1
  165.4 1.5 fusion.85
  166.9 0.8 fusion.88
  167.7 1.8 gather_fusion.1
  169.6 1.5 fusion.85
  171.2 0.8 fusion.88
  172.0 1.8 gather_fusion.1
  173.8 1.5 fusion.85
  175.4 0.8 fusion.88
  176.2 1.8 gather_fusion.1
  178.0 1.5 fusion.85
  179.6 0.8 fusion.88
  180.4 1.8 gather_fusion.1
  182.3 1.5 fusion.85
  183.8 0.8 fusion.88
  184.7 1.8 gather_fusion.1
  186.5 1.5 fusion.85
  188.1 0.8 fusion.88
  188.9 1.1 copy.25
  190.0 20.4 %reduce-scatter.5.cloned.1.call-done = bf16[256,256]{1,0:T(8,128)(2,1)} async-done(((bf16[1024,256]{1,0:T(8,128)(2,1)}), bf16[256,256]{1,0:T(8,128)(2,1)}) %reduce-scatter.5.cloned.1.call-update) | async-done | bytes 131088 | tf_op jit(solution)/shard_map/reduce_scatter | solution.py:91
  210.5 1.8 convolution_bitcast_fusion
  212.3 1.8 convolution_convert_fusion
  214.1 128.9 %all-reduce.2.cloned.1.call-done = f32[256,256]{0,1:T(8,128)} async-done(((f32[256,256]{0,1:T(8,128)}), f32[256,256]{0,1:T(8,128)}) %all-reduce.2.cloned.1.call-update) | async-done | bytes 262160 | tf_op jit(solution)/shard_map/psum | solution.py:97
  343.0 1.8 copy.13
  (72 shorter events, 3.8 us)
Async XLA Ops:
  7.2 2.7 copy-start
  7.2 114.3 %reduce-scatter.3.cloned.1.call-start = ((), (), s32[]{:S(2)}) async-start(), calls=%async_computation.2 | async-start | bytes 1179648 | tf_op jit(solution)/shard_map/reduce_scatter | solution.py:79
  54.9 66.5 %copy-start.2 = (bf16[256,256]{1,0:T(8,128)(2,1)S(1)}, bf16[256,256]{1,0:T(8,128)(2,1)}, u32[]{:S(2)}) copy-start(bf16[256,256]{1,0:T(8,128)(2,1)} %param.12) | copy-start | bytes 393220
  56.3 107.2 %all-gather.2.cloned.1.call-start = ((), (), s32[]{:S(2)}) async-start(), calls=%async_computation.3 | async-start | bytes 1179648 | tf_op jit(solution)/shard_map/all_gather | solution.py:87
  123.2 87.3 %reduce-scatter.5.cloned.1.call-start = ((), (), s32[]{:S(2)}) async-start(), calls=%async_computation.4 | async-start | bytes 655360 | tf_op jit(solution)/shard_map/reduce_scatter | solution.py:91
  188.8 23.5 %copy-start.1 = (bf16[256,256]{1,0:T(8,128)(2,1)S(1)}, bf16[256,256]{1,0:T(8,128)(2,1)}, u32[]{:S(2)}) copy-start(bf16[256,256]{1,0:T(8,128)(2,1)} %param.11) | copy-start | bytes 393220
  190.0 153.0 %all-reduce.2.cloned.1.call-start = ((), (), s32[]{:S(2)}) async-start(), calls=%async_computation.5 | async-start | bytes 524288 | tf_op jit(solution)/shard_map/psum | solution.py:97
Sparse Core Ops, SparseCore 0:
  56.4 64.9 reduce-scatter.2
  124.2 39.3 all-gather.1
  190.1 20.3 reduce-scatter.4
  216.4 126.5 all-reduce.1
where the time goes:
time: 353 us; the launch traced here: 351 us
  waiting for transfers between devices  255 us (72%)
  matrix products  47.9 us (14%)
  local copies, waits for them, and re-layouts  19.8 us (6%)
  between operations  14.5 us (4%)
  blocking collectives  8.65 us (2%)
  other arithmetic  4.97 us (1%)
    psum x1, waiting for transfers between devices, body(): grad_weight = lax.psum(local_weight, ('row', 'col'))  129 us
    reduce_scatter x1, waiting for transfers between devices, body(): lax.psum_scatter(partial_value.astype(jnp.bfloat16), 'col', scatter_dimen...  65.1 us
    all_gather x1, waiting for transfers between devices, body(): grad_panel = lax.all_gather(grad_hidden, 'col', axis=0, tiled=True)  40.2 us
    dot_general x6, matrix products, step(): return (totals + jnp.einsum('bk,kif->bif', onehot, prod), None)  20.7 us
    reduce_scatter x1, waiting for transfers between devices, body(): lax.psum_scatter(partial_back.astype(jnp.bfloat16), 'row', scatter_dimens...  20.4 us
    gather x6, local copies, waits for them, and re-layouts, step(): picked = blocks[rows_idx]  11 us
    dot_general x6, matrix products, step(): jnp.einsum('kij,kif->kjf', vals, picked, preferred_element_type=jnp.float32)  9.18 us
    dot_general x6, matrix products, step(): jnp.einsum('kij,kjf->kif', vals, picked, preferred_element_type=jnp.float32)  8.8 us
  transfers between devices with their start and end apart: 4, of which 4 were waited for; matrix products, arithmetic and copies ran while one was open for 1% of the time, Pallas kernels for 0%

commit v1 on v0

v1 whole, which is shorter than its diff:
```python
import functools

import jax
import jax.numpy as jnp
from jax import lax
from jax.experimental import pallas as pl
from jax.experimental.pallas import tpu as pltpu
from jax.sharding import PartitionSpec as P

MESH = pl.DeviceIdType.MESH
F32 = jnp.float32
BF16 = jnp.bfloat16


def split_axis(size, inner):
    while size % inner:
        inner -= 1
    return size // inner, inner


def kernel(
    dims,
    inv_ref,
    feat_ref,
    weight_ref,
    gout_ref,
    adj_ref,
    act_ref,
    gin_ref,
    gw_ref,
    vals,
    dense,
    dense_t,
    feats,
    feats_t,
    xw,
    wbuf,
    gout,
    cs_y,
    cr_y,
    cs_z,
    cr_z,
    ghs,
    acc,
    rs_y,
    rr_y,
    rs_z,
    rr_z,
    ws,
    wr,
    w2,
    w3,
    local_sem,
    sem_f,
    sem_fr,
    sem_cy,
    sem_cz,
    sem_g,
    sem_gr,
    sem_ry,
    sem_rz,
    sem_w1,
    sem_w2,
    sem_w2r,
    sem_w3,
    sem_w3r,
):
    (nrow, ncol, ro, ri, co, ci) = dims
    slots, bs, _ = adj_ref.shape
    own, width = feat_ref.shape
    row_blocks = dense.shape[0] // bs
    col_blocks = dense.shape[1] // bs
    row = lax.axis_index("row")
    col = lax.axis_index("col")
    rx, rc = lax.div(row, ri), lax.rem(row, ri)
    cz, cy = lax.div(col, ci), lax.rem(col, ci)

    def remote(src, dst, send, recv, axis, peer):
        return pltpu.make_async_remote_copy(
            src_ref=src,
            dst_ref=dst,
            send_sem=send,
            recv_sem=recv,
            device_id={axis: peer},
            device_id_type=MESH,
        )

    loads = [
        pltpu.make_async_copy(feat_ref, feats.at[row], local_sem.at[0]),
        pltpu.make_async_copy(weight_ref, wbuf, local_sem.at[1]),
        pltpu.make_async_copy(adj_ref, vals.at[pl.ds(0, slots)], local_sem.at[2]),
        pltpu.make_async_copy(gout_ref, gout, local_sem.at[3]),
    ]
    for load in loads:
        load.start()

    barrier = pltpu.get_barrier_semaphore()
    for d in range(1, nrow):
        pl.semaphore_signal(
            barrier, inc=1, device_id={"row": lax.rem(row + d, nrow)}, device_id_type=MESH
        )
    for d in range(1, ncol):
        pl.semaphore_signal(
            barrier, inc=1, device_id={"col": lax.rem(col + d, ncol)}, device_id_type=MESH
        )
    vals[slots] = jnp.zeros((bs, bs), vals.dtype)
    loads[0].wait()
    pl.semaphore_wait(barrier, nrow + ncol - 2)

    def gather(axis, buf, outer, inner, n_out, n_in, send, recv, hook):
        me = outer * n_in + inner
        started = []
        slot = 0

        def push(block, peer):
            copy = remote(
                buf.at[block], buf.at[block], send.at[len(started)], recv.at[block], axis, peer
            )
            copy.start()
            started.append(copy)

        def arrive(block):
            remote(buf.at[block], buf.at[block], send.at[0], recv.at[block], axis, me).wait_recv()

        for d in range(n_out - 1, 0, -1):
            push(me, lax.rem(outer + d, n_out) * n_in + inner)
        for e in range(1, n_in):
            push(me, outer * n_in + lax.rem(inner + e, n_in))
        hook(me)
        for d in range(1, n_out):
            source = lax.rem(outer + d, n_out)
            block = source * n_in + inner
            arrive(block)
            for e in range(1, n_in):
                push(block, outer * n_in + lax.rem(inner + e, n_in))
            hook(block)
        for d in range(n_out):
            source = lax.rem(outer + d, n_out)
            for e in range(1, n_in):
                block = source * n_in + lax.rem(inner + n_in - e, n_in)
                arrive(block)
                hook(block)
        return started

    def rows(block):
        return pl.ds(pl.multiple_of(block * own, own), own)

    def project(block):
        xw[rows(block), :] = jnp.dot(
            feats[block], wbuf[...], preferred_element_type=F32
        ).astype(BF16)
        feats_t[:, rows(block)] = feats[block].T

    def first(block):
        loads[1].wait()
        loads[2].wait()

        def fill(r, carry):
            for c in range(col_blocks):
                tile = vals[inv_ref[r * col_blocks + c]]
                at = pl.ds(pl.multiple_of(r * bs, bs), bs)
                dense[at, c * bs : (c + 1) * bs] = tile
                dense_t[c * bs : (c + 1) * bs, at] = tile.T
            return carry

        lax.fori_loop(0, row_blocks, fill, 0)
        project(block)

    calls = [first]

    def feature_hook(block):
        (calls.pop() if calls else project)(block)

    pending = gather("row", feats, rx, rc, ro, ri, sem_f, sem_fr, feature_hook)

    def reduce_start(axis, part, outer, inner, n_out, n_in, s_in, r_in, sems):
        copies = []
        for d in list(range(1, n_out)) + [0]:
            to = lax.rem(outer + d, n_out)
            for e in range(1, n_in):
                peer = lax.rem(inner + e, n_in)
                slot = d * (n_in - 1) + e - 1
                s_in[slot] = part(to * n_in + peer).astype(BF16)
                copy = remote(
                    s_in.at[slot],
                    r_in.at[to * (n_in - 1) + e - 1],
                    sems.at[0, slot],
                    sems.at[1, to * (n_in - 1) + e - 1],
                    axis,
                    outer * n_in + peer,
                )
                copy.start()
                copies.append(copy)
        return copies

    def reduce_middle(axis, part, outer, inner, n_out, n_in, r_in, s_out, r_out, sem_i, sem_o):
        copies = []
        total = None
        for d in list(range(1, n_out)) + [0]:
            to = lax.rem(outer + d, n_out)
            value = part(to * n_in + inner)
            for e in range(1, n_in):
                at = to * (n_in - 1) + e - 1
                remote(
                    r_in.at[at], r_in.at[at], sem_i.at[0, 0], sem_i.at[1, at], axis, 0
                ).wait_recv()
                value = value + r_in[at].astype(F32)
            if d == 0:
                total = value
            else:
                s_out[d - 1] = value.astype(BF16)
                copy = remote(
                    s_out.at[d - 1],
                    r_out.at[d - 1],
                    sem_o.at[0, d - 1],
                    sem_o.at[1, d - 1],
                    axis,
                    to * n_in + inner,
                )
                copy.start()
                copies.append(copy)
        return copies, total

    def reduce_end(total, copies, r_out):
        for d, copy in enumerate(copies):
            copy.wait_recv()
            total = total + r_out[d].astype(F32)
        return total

    def forward(block):
        return jnp.dot(dense[rows(block), :], xw[...], preferred_element_type=F32)

    pending += reduce_start("col", forward, cz, cy, co, ci, cs_y, cr_y, sem_cy)
    copies, total = reduce_middle(
        "col", forward, cz, cy, co, ci, cr_y, cs_z, cr_z, sem_cy, sem_cz
    )
    hidden = reduce_end(total, copies, cr_z)
    pending += copies
    loads[3].wait()
    sigma = jax.nn.sigmoid(hidden)
    ghs[col] = (gout[...].astype(F32) * sigma * (1.0 + hidden * (1.0 - sigma))).astype(BF16)
    act_ref[...] = (hidden * sigma).astype(BF16)

    seen = []

    def backward(block):
        term = jnp.dot(dense_t[:, rows(block)], ghs[block], preferred_element_type=F32)
        acc[...] = acc[...] + term if seen else term
        seen.append(1)

    pending += gather("col", ghs, cz, cy, co, ci, sem_g, sem_gr, backward)

    grad = jnp.dot(feats_t[...], acc[...].astype(BF16), preferred_element_type=F32)
    part_rows = width // ncol
    ws[...] = grad.astype(BF16).reshape(ncol, part_rows, width)
    w1 = []
    for d in range(1, ncol):
        peer = lax.rem(col + d, ncol)
        copy = remote(
            ws.at[peer], wr.at[d - 1], sem_w1.at[0, d - 1], sem_w1.at[1, d - 1], "col", peer
        )
        copy.start()
        w1.append(copy)

    def back(block):
        return acc[rows(block), :]

    pending += reduce_start("row", back, rx, rc, ro, ri, rs_y, rr_y, sem_ry)
    copies, total = reduce_middle(
        "row", back, rx, rc, ro, ri, rr_y, rs_z, rr_z, sem_ry, sem_rz
    )
    pending += copies

    share = ws[col].astype(F32)
    for d, copy in enumerate(w1):
        copy.wait_recv()
        share = share + wr[d].astype(F32)
    w2[row] = share.astype(BF16)
    w2_copies = []
    for d in range(1, nrow):
        copy = remote(
            w2.at[row], w2.at[row], sem_w2.at[d - 1], sem_w2r.at[row], "row", lax.rem(row + d, nrow)
        )
        copy.start()
        w2_copies.append(copy)

    grad_xw = reduce_end(total, copies, rr_z).astype(BF16)
    gin_ref[...] = lax.dot_general(
        grad_xw, wbuf[...], (((1,), (1,)), ((), ())), preferred_element_type=F32
    ).astype(BF16)

    for d in range(1, nrow):
        source = lax.rem(row + d, nrow)
        remote(
            w2.at[source], w2.at[source], sem_w2.at[0], sem_w2r.at[source], "row", source
        ).wait_recv()
    share = w2[0].astype(F32)
    for d in range(1, nrow):
        share = share + w2[d].astype(F32)
    w3[col] = share.astype(BF16)
    w3_copies = []
    for d in range(1, ncol):
        copy = remote(
            w3.at[col], w3.at[col], sem_w3.at[d - 1], sem_w3r.at[col], "col", lax.rem(col + d, ncol)
        )
        copy.start()
        w3_copies.append(copy)
    for d in range(1, ncol):
        source = lax.rem(col + d, ncol)
        remote(
            w3.at[source], w3.at[source], sem_w3.at[0], sem_w3r.at[source], "col", source
        ).wait_recv()
    gw_ref[...] = w3[...].astype(F32).reshape(width, width)
    for copy in pending + w1 + w2_copies + w3_copies:
        copy.wait_send()


def solution(mesh):
    nrow, ncol = mesh.shape["row"], mesh.shape["col"]
    ro, ri = split_axis(nrow, 2)
    zs = 4 if ncol % 4 == 0 else 1
    co, ci = zs, ncol // zs
    dims = (nrow, ncol, ro, ri, co, ci)

    def body(features, weight, grad_out, adj_values, block_pos, block_count):
        own, width = features.shape
        slots, bs, _ = adj_values.shape
        rows_tile = own * ncol
        cols_tile = own * nrow
        spots = (rows_tile // bs) * (cols_tile // bs)
        order = jnp.arange(slots, dtype=jnp.int32)
        hit = (block_pos[0][None, :] == jnp.arange(spots, dtype=jnp.int32)[:, None]) & (
            order < block_count[0, 0]
        )[None, :]
        inv = slots + jnp.sum(jnp.where(hit, order - slots, 0), axis=1)
        block = lambda n: pltpu.VMEM((max(n, 1), own, width), BF16)
        dma = pltpu.SemaphoreType.DMA
        part_rows = width // ncol

        def ag_sends(o, i):
            return max((o - 1) + (i - 1) + (o - 1) * (i - 1), 1)

        scratch = [
            pltpu.VMEM((slots + 1, bs, bs), BF16),
            pltpu.VMEM((rows_tile, cols_tile), BF16),
            pltpu.VMEM((cols_tile, rows_tile), BF16),
            block(nrow),
            pltpu.VMEM((width, cols_tile), BF16),
            pltpu.VMEM((cols_tile, width), BF16),
            pltpu.VMEM((width, width), BF16),
            pltpu.VMEM((own, width), BF16),
            block(co * (ci - 1)),
            block(co * (ci - 1)),
            block(co - 1),
            block(co - 1),
            block(ncol),
            pltpu.VMEM((cols_tile, width), F32),
            block(ro * (ri - 1)),
            block(ro * (ri - 1)),
            block(ro - 1),
            block(ro - 1),
            pltpu.VMEM((ncol, part_rows, width), BF16),
            pltpu.VMEM((ncol, part_rows, width), BF16),
            pltpu.VMEM((nrow, part_rows, width), BF16),
            pltpu.VMEM((ncol, part_rows, width), BF16),
            dma((4,)),
            dma((ag_sends(ro, ri),)),
            dma((nrow,)),
            dma((2, max(co * (ci - 1), 1))),
            dma((2, max(co - 1, 1))),
            dma((ag_sends(co, ci),)),
            dma((ncol,)),
            dma((2, max(ro * (ri - 1), 1))),
            dma((2, max(ro - 1, 1))),
            dma((2, ncol)),
            dma((nrow,)),
            dma((nrow,)),
            dma((ncol,)),
            dma((ncol,)),
        ]
        anyspace = pl.BlockSpec(memory_space=pl.ANY)
        return pl.pallas_call(
            functools.partial(kernel, dims),
            out_shape=(
                jax.ShapeDtypeStruct((own, width), BF16),
                jax.ShapeDtypeStruct((own, width), BF16),
                jax.ShapeDtypeStruct((width, width), F32),
            ),
            in_specs=[pl.BlockSpec(memory_space=pltpu.SMEM)] + [anyspace] * 4,
            out_specs=[pl.BlockSpec(memory_space=pltpu.VMEM)] * 3,
            scratch_shapes=scratch,
            compiler_params=pltpu.CompilerParams(
                collective_id=0,
                has_side_effects=True,
                vmem_limit_bytes=66 * 1000 * 1000,
            ),
        )(inv, features, weight, grad_out, adj_values)

    placed = (
        P(("col", "row"), None),
        P(),
        P(("row", "col"), None),
        P("row", "col", None),
        P("row", "col"),
        P("row", "col"),
    )
    return jax.shard_map(
        body,
        mesh=mesh,
        in_specs=placed,
        out_specs=(P(("row", "col"), None), P(("col", "row"), None), P()),
        check_vma=False,
    )
```

time: 353 us -> 72.7 us (0.21)
  waiting for transfers between devices: 255 us -> 0 us
  Pallas kernels: 0 us -> 65.1 us
  matrix products: 47.9 us -> 0 us
  local copies, waits for them, and re-layouts: 19.8 us -> 4.8 us
  between operations: 14.5 us -> 1.3 us
  blocking collectives: 8.65 us -> 0 us
  other arithmetic: 4.97 us -> 1.3 us
    psum x1 -> x0, waiting for transfers between devices: 129 us -> none  [body(): grad_weight = lax.psum(local_weight, ('row', 'col'))]
    reduce_scatter x2 -> x0, waiting for transfers between devices: 85.5 us -> none  [the longest x1 65.1 us: body(): lax.psum_scatter(partial_value.astype(jnp.bfloat16), 'col', scatter_dimen...]
    pallas_call x0 -> x1, Pallas kernels: none -> 65.1 us  [body(): pl.pallas_call(functools.partial(kernel, dims), out_shape=(jax.ShapeDtype...]
    dot_general x27 -> x0, matrix products: 47.9 us -> none  [the longest x6 20.7 us: step(): return (totals + jnp.einsum('bk,kif->bif', onehot, prod), None)]
    all_gather x1 -> x0, waiting for transfers between devices: 40.2 us -> none  [body(): grad_panel = lax.all_gather(grad_hidden, 'col', axis=0, tiled=True)]
    gather x12 -> x0, local copies, waits for them, and re-layouts: 14.7 us -> none  [the longest x6 11 us: step(): picked = blocks[rows_idx]]
    all_gather x1 -> x0, blocking collectives: 8.65 us -> none  [body(): panel = lax.all_gather(projected, 'row', axis=0, tiled=True)]
  transfers between devices with their start and end apart: 4 -> 0, of which waited for: 4 -> 0; matrix products, arithmetic and copies ran while one was open for 1% -> 0% of each run, Pallas kernels for 0% -> 0%
where the time goes in v1:
time: 72.7 us; the launch traced here: 72.5 us
  Pallas kernels  65.1 us (90%)
  local copies, waits for them, and re-layouts  4.8 us (7%)
  other arithmetic  1.3 us (2%)
  between operations  1.3 us (2%)
    pallas_call x1, Pallas kernels, body(): pl.pallas_call(functools.partial(kernel, dims), out_shape=(jax.ShapeDtype...  65.1 us
    unnamed x3, local copies, waits for them, and re-layouts  4.8 us

profile of v1, /device:TPU:0, one launch (start us, length us, event | category | flops | bytes accessed | tf_op | source)
XLA Modules:
  0.0 72.5 jit_solution(7713891528196283957)
XLA Ops:
  1.3 0.8 %select_reduce_fusion = s32[128]{0:T(128)S(1)} fusion(s32[96]{0:T(128)S(1)} %iota_add_fusion, s32[96]{0:T(128)} %bitcast.3, pred[96]{0:T(512)(128)(4,1)S(1)} %iota_compare_fusion.1), kind=kLoop, calls=%fused_computation | loop fusion | flops 49024 | bytes 1376 | tf_op jit(solution)/shard_map/reduce_sum | solution.py:335
  2.1 0.5 broadcast_add_fusion.inv_ref
  2.6 65.1 %shard_map.85 = (bf16[256,256]{1,0:T(8,128)(2,1)}, bf16[256,256]{1,0:T(8,128)(2,1)}, f32[256,256]{1,0:T(8,128)}) custom-call(s32[128]{0:T(128)} %broadcast_add_fusion.inv_ref, bf16[256,256]{1,0:T(8,128)(2,1)} %feat_ref.1, bf16[256,256]{1,0:T(8,128)(2,1)} %weight_ref.1, bf16[256,256]{1,0:T(8,128)(2,1)} %gout_ref.1, bf16[96,128,128]{2,1,0:T(8,128)(2,1)} %adj_ref.1), custom_call_target="tpu_custom_call" | custom-call | tf_op jit(solution)/shard_map/pallas_call | solution.py:382
  67.7 1.6 %copy.13 = bf16[256,256]{1,0:T(8,128)(2,1)} copy(bf16[256,256]{1,0:T(8,128)(2,1)} %get-tuple-element.6) | data formatting | bytes 262144
  69.2 1.6 %copy.14 = bf16[256,256]{1,0:T(8,128)(2,1)} copy(bf16[256,256]{1,0:T(8,128)(2,1)} %get-tuple-element.7) | data formatting | bytes 262144
  70.8 1.7 %copy.15 = f32[256,256]{1,0:T(8,128)} copy(f32[256,256]{1,0:T(8,128)} %get-tuple-element.8) | data formatting | bytes 524288
  (2 shorter events, 0.0 us)

commit v2 on v0

v2 whole, which is shorter than its diff:
```python
import functools

import jax
import jax.numpy as jnp
from jax import lax
from jax.experimental import pallas as pl
from jax.experimental.pallas import tpu as pltpu
from jax.sharding import PartitionSpec as P

MESH = pl.DeviceIdType.MESH
F32 = jnp.float32
BF16 = jnp.bfloat16


def split_axis(size, inner):
    while size % inner:
        inner -= 1
    return size // inner, inner


class Reduce:
    def __init__(self, link, axis, outer, inner, n_out, n_in, part, bufs, sems):
        self.link, self.axis, self.part = link, axis, part
        self.outer, self.inner, self.n_out, self.n_in = outer, inner, n_out, n_in
        self.s_in, self.r_in, self.s_out, self.r_out = bufs
        self.sem_in, self.sem_out = sems
        self.sent, self.totals = [], {}

    def to(self, d):
        return lax.rem(self.outer + d, self.n_out)

    def start(self, h, d):
        to = self.to(d)
        for e in range(1, self.n_in):
            peer = lax.rem(self.inner + e, self.n_in)
            slot = (h * self.n_out + d) * (self.n_in - 1) + e - 1
            there = (h * self.n_out + to) * (self.n_in - 1) + e - 1
            self.s_in[slot] = self.part(to * self.n_in + peer, h).astype(BF16)
            copy = self.link(
                self.s_in.at[slot],
                self.r_in.at[there],
                self.sem_in.at[0, slot],
                self.sem_in.at[1, there],
                self.axis,
                self.outer * self.n_in + peer,
            )
            copy.start()
            self.sent.append(copy)

    def middle(self, h, d):
        to = self.to(d)
        value = self.part(to * self.n_in + self.inner, h)
        for e in range(1, self.n_in):
            at = (h * self.n_out + to) * (self.n_in - 1) + e - 1
            self.link(
                self.r_in.at[at],
                self.r_in.at[at],
                self.sem_in.at[0, 0],
                self.sem_in.at[1, at],
                self.axis,
                0,
            ).wait_recv()
            value = value + self.r_in[at].astype(F32)
        if d == 0:
            self.totals[h] = value
            return
        slot = h * (self.n_out - 1) + d - 1
        self.s_out[slot] = value.astype(BF16)
        copy = self.link(
            self.s_out.at[slot],
            self.r_out.at[slot],
            self.sem_out.at[0, slot],
            self.sem_out.at[1, slot],
            self.axis,
            to * self.n_in + self.inner,
        )
        copy.start()
        self.sent.append(copy)

    def end(self, h):
        total = self.totals[h]
        for d in range(1, self.n_out):
            slot = h * (self.n_out - 1) + d - 1
            self.link(
                self.r_out.at[slot],
                self.r_out.at[slot],
                self.sem_out.at[0, slot],
                self.sem_out.at[1, slot],
                self.axis,
                0,
            ).wait_recv()
            total = total + self.r_out[slot].astype(F32)
        return total


class Gather:
    def __init__(self, link, axis, outer, inner, n_out, n_in, halves, buf, send, recv):
        self.link, self.axis, self.halves = link, axis, halves
        self.outer, self.inner, self.n_out, self.n_in = outer, inner, n_out, n_in
        self.buf, self.send, self.recv = buf, send, recv
        self.me = outer * n_in + inner
        self.sent = []

    def push(self, block, h, peer):
        at = block * self.halves + h
        copy = self.link(
            self.buf.at[at],
            self.buf.at[at],
            self.send.at[len(self.sent)],
            self.recv.at[at],
            self.axis,
            peer,
        )
        copy.start()
        self.sent.append(copy)

    def arrive(self, block, h):
        at = block * self.halves + h
        self.link(
            self.buf.at[at], self.buf.at[at], self.send.at[0], self.recv.at[at], self.axis, 0
        ).wait_recv()

    def forward(self, block, h):
        for e in range(1, self.n_in):
            self.push(block, h, self.outer * self.n_in + lax.rem(self.inner + e, self.n_in))

    def start(self, h):
        for d in range(self.n_out - 1, 0, -1):
            self.push(self.me, h, lax.rem(self.outer + d, self.n_out) * self.n_in + self.inner)
        self.forward(self.me, h)

    def from_outer(self, h, d):
        block = lax.rem(self.outer + d, self.n_out) * self.n_in + self.inner
        self.arrive(block, h)
        self.forward(block, h)
        return [block]

    def from_inner(self, h, d):
        blocks = []
        for e in range(1, self.n_in):
            block = lax.rem(self.outer + d, self.n_out) * self.n_in + lax.rem(
                self.inner + e, self.n_in
            )
            self.arrive(block, h)
            blocks.append(block)
        return blocks


def kernel(
    dims,
    count_ref,
    pos_ref,
    feat_ref,
    weight_ref,
    gout_ref,
    adj_ref,
    act_ref,
    gin_ref,
    gw_ref,
    inv_v,
    inv_s,
    vals,
    dense,
    dense_t,
    feats,
    wbuf,
    gout,
    cs_y,
    cr_y,
    cs_z,
    cr_z,
    af,
    ghs,
    acc,
    rs_y,
    rr_y,
    rs_z,
    rr_z,
    ws1,
    wr1,
    ws2,
    wr2,
    w4,
    local_sem,
    sem_f,
    sem_fr,
    sem_cy,
    sem_cz,
    sem_g,
    sem_gr,
    sem_ry,
    sem_rz,
    sem_w1,
    sem_w2,
    sem_w3,
    sem_w3r,
    sem_w4,
    sem_w4r,
):
    (nrow, ncol, ro, ri, co, ci, halves) = dims
    slots, bs, _ = adj_ref.shape
    own, width = feat_ref.shape
    half = own // halves
    row_blocks = dense.shape[0] // bs
    col_blocks = dense.shape[1] // bs
    spots = row_blocks * col_blocks
    row = lax.axis_index("row")
    col = lax.axis_index("col")
    rx, rc = lax.div(row, ri), lax.rem(row, ri)
    cz, cy = lax.div(col, ci), lax.rem(col, ci)

    def remote(src, dst, send, recv, axis, peer):
        return pltpu.make_async_remote_copy(
            src_ref=src,
            dst_ref=dst,
            send_sem=send,
            recv_sem=recv,
            device_id={axis: peer},
            device_id_type=MESH,
        )

    loads = [
        pltpu.make_async_copy(feat_ref, feats.at[row], local_sem.at[0]),
        pltpu.make_async_copy(adj_ref, vals.at[pl.ds(0, slots)], local_sem.at[1]),
        pltpu.make_async_copy(weight_ref, wbuf, local_sem.at[2]),
        pltpu.make_async_copy(gout_ref, gout, local_sem.at[3]),
    ]
    for load in loads:
        load.start()

    barrier = pltpu.get_barrier_semaphore()
    for d in range(1, nrow):
        pl.semaphore_signal(
            barrier, inc=1, device_id={"row": lax.rem(row + d, nrow)}, device_id_type=MESH
        )
    for d in range(1, ncol):
        pl.semaphore_signal(
            barrier, inc=1, device_id={"col": lax.rem(col + d, ncol)}, device_id_type=MESH
        )
    slot = lax.broadcasted_iota(jnp.int32, (spots, slots), 1)
    spot = lax.broadcasted_iota(jnp.int32, (spots, slots), 0)
    hit = (pos_ref[...] == spot) & (slot < count_ref[0, 0])
    found = slots + jnp.sum(jnp.where(hit, slot - slots, 0), axis=1, keepdims=True)
    inv_v[...] = jnp.broadcast_to(found, (spots, 128)).T[:8]
    table = pltpu.make_async_copy(inv_v, inv_s, local_sem.at[4])
    table.start()
    vals[slots] = jnp.zeros((bs, bs), vals.dtype)
    loads[0].wait()
    pl.semaphore_wait(barrier, nrow + ncol - 2)

    g1 = Gather(remote, "row", rx, rc, ro, ri, 1, feats, sem_f, sem_fr)
    g1.start(0)
    table.wait()
    loads[1].wait()

    def fill(r, carry):
        for c in range(col_blocks):
            tile = vals[inv_s[0, r * col_blocks + c]]
            at = pl.ds(pl.multiple_of(r * bs, bs), bs)
            dense[at, c * bs : (c + 1) * bs] = tile
            dense_t[c * bs : (c + 1) * bs, at] = tile.T
        return carry

    lax.fori_loop(0, row_blocks, fill, 0)
    for d in range(1, ro):
        g1.from_outer(0, d)
    for d in range(ro):
        g1.from_inner(0, d)

    def rows(block, h=0, size=own):
        return pl.ds(pl.multiple_of(block * own + h * size, size), size)

    def forward(block, h):
        return jnp.dot(
            dense[rows(block, h, half), :],
            feats[...].reshape(nrow * own, width),
            preferred_element_type=F32,
        )

    rsc = Reduce(
        remote, "col", cz, cy, co, ci, forward, (cs_y, cr_y, cs_z, cr_z), (sem_cy, sem_cz)
    )
    agc = Gather(remote, "col", cz, cy, co, ci, halves, ghs, sem_g, sem_gr)
    order = list(range(1, co)) + [0]
    for h in range(halves):
        for d in order:
            rsc.start(h, d)
    loads[2].wait()
    loads[3].wait()

    def owner(h):
        piece = rsc.end(h).astype(BF16)
        at = slice(h * half, (h + 1) * half)
        af[at, :] = piece
        hidden = jnp.dot(piece, wbuf[...], preferred_element_type=F32)
        sigma = jax.nn.sigmoid(hidden)
        ghs[col * halves + h] = (
            gout[at, :].astype(F32) * sigma * (1.0 + hidden * (1.0 - sigma))
        ).astype(BF16)
        agc.start(h)
        act_ref[at, :] = (hidden * sigma).astype(BF16)

    for d in order:
        rsc.middle(0, d)
    for h in range(1, halves):
        for d in order[:-1]:
            rsc.middle(h, d)
        owner(h - 1)
        rsc.middle(h, 0)
    owner(halves - 1)

    grad = jnp.dot(
        af[...].T,
        ghs[pl.ds(col * halves, halves)].reshape(own, width),
        preferred_element_type=F32,
    )
    rows1 = width // nrow
    rows2 = rows1 // ncol
    ws1[...] = grad.astype(BF16).reshape(nrow, rows1, width)
    w1 = []
    for d in range(1, nrow):
        peer = lax.rem(row + d, nrow)
        copy = remote(
            ws1.at[peer], wr1.at[d - 1], sem_w1.at[0, d - 1], sem_w1.at[1, d - 1], "row", peer
        )
        copy.start()
        w1.append(copy)

    seen = []

    def backward(blocks):
        for block in blocks:
            term = jnp.dot(
                dense_t[:, rows(block)],
                ghs[pl.ds(block * halves, halves)].reshape(own, width),
                preferred_element_type=F32,
            )
            acc[...] = acc[...] + term if seen else term
            seen.append(1)

    last = halves - 1
    for h in range(last):
        for d in range(1, co):
            agc.from_outer(h, d)
    backward([agc.me])

    share = ws1[row].astype(F32)
    for d, copy in enumerate(w1):
        copy.wait_recv()
        share = share + wr1[d].astype(F32)
    for k in range(ncol):
        ws2[k] = share[k * rows2 : (k + 1) * rows2].astype(BF16)
    w2 = []
    for d in range(1, ncol):
        peer = lax.rem(col + d, ncol)
        copy = remote(
            ws2.at[peer], wr2.at[d - 1], sem_w2.at[0, d - 1], sem_w2.at[1, d - 1], "col", peer
        )
        copy.start()
        w2.append(copy)

    for d in range(1, co):
        backward(agc.from_outer(last, d))
    for h in range(last):
        for d in range(co):
            agc.from_inner(h, d)

    share = ws2[col].astype(F32)
    for d, copy in enumerate(w2):
        copy.wait_recv()
        share = share + wr2[d].astype(F32)
    w4[row, col] = share.astype(BF16)
    w3 = []
    for d in range(1, ncol):
        peer = lax.rem(col + d, ncol)
        copy = remote(
            w4.at[row, col], w4.at[row, col], sem_w3.at[d - 1], sem_w3r.at[col], "col", peer
        )
        copy.start()
        w3.append(copy)

    for d in range(co):
        backward(agc.from_inner(last, d))

    def back(block, h):
        return acc[rows(block), :]

    rsr = Reduce(
        remote, "row", rx, rc, ro, ri, back, (rs_y, rr_y, rs_z, rr_z), (sem_ry, sem_rz)
    )
    order = list(range(1, ro)) + [0]
    for d in order:
        rsr.start(0, d)

    for d in range(1, ncol):
        source = lax.rem(col + d, ncol)
        remote(
            w4.at[row, source], w4.at[row, source], sem_w3.at[0], sem_w3r.at[source], "col", source
        ).wait_recv()
    w4c = []
    for d in range(1, nrow):
        peer = lax.rem(row + d, nrow)
        copy = remote(w4.at[row], w4.at[row], sem_w4.at[d - 1], sem_w4r.at[row], "row", peer)
        copy.start()
        w4c.append(copy)

    for d in order:
        rsr.middle(0, d)
    for d in range(1, nrow):
        source = lax.rem(row + d, nrow)
        remote(
            w4.at[source], w4.at[source], sem_w4.at[0], sem_w4r.at[source], "row", source
        ).wait_recv()
    for r in range(nrow):
        for k in range(ncol):
            at = r * rows1 + k * rows2
            gw_ref[at : at + rows2, :] = w4[r, k].astype(F32)
    gin_ref[...] = lax.dot_general(
        rsr.end(0).astype(BF16), wbuf[...], (((1,), (1,)), ((), ())), preferred_element_type=F32
    ).astype(BF16)
    for copy in g1.sent + rsc.sent + agc.sent + rsr.sent + w1 + w2 + w3 + w4c:
        copy.wait_send()


def hand_on(a_in, b_in, c_in, a_out, b_out, c_out):
    a_out[...] = a_in[...]
    b_out[...] = b_in[...]
    c_out[...] = c_in[...]


def solution(mesh):
    nrow, ncol = mesh.shape["row"], mesh.shape["col"]
    ro, ri = split_axis(nrow, 2)
    co = 4 if ncol % 4 == 0 else 1
    ci = ncol // co
    halves = 2
    dims = (nrow, ncol, ro, ri, co, ci, halves)

    def body(features, weight, grad_out, adj_values, block_pos, block_count):
        own, width = features.shape
        slots, bs, _ = adj_values.shape
        rows_tile = own * ncol
        cols_tile = own * nrow
        spots = (rows_tile // bs) * (cols_tile // bs)
        half = own // halves
        rows1 = width // nrow
        rows2 = rows1 // ncol
        dma = pltpu.SemaphoreType.DMA

        def block(n, rows):
            return pltpu.VMEM((max(n, 1), rows, width), BF16)

        def ag_sends(o, i):
            return max((o - 1) + (i - 1) + (o - 1) * (i - 1), 1)

        scratch = [
            pltpu.VMEM((8, spots), jnp.int32),
            pltpu.SMEM((8, spots), jnp.int32),
            pltpu.VMEM((slots + 1, bs, bs), BF16),
            pltpu.VMEM((rows_tile, cols_tile), BF16),
            pltpu.VMEM((cols_tile, rows_tile), BF16),
            block(nrow, own),
            pltpu.VMEM((width, width), BF16),
            pltpu.VMEM((own, width), BF16),
            block(halves * co * (ci - 1), half),
            block(halves * co * (ci - 1), half),
            block(halves * (co - 1), half),
            block(halves * (co - 1), half),
            pltpu.VMEM((own, width), BF16),
            block(ncol * halves, half),
            pltpu.VMEM((cols_tile, width), F32),
            block(ro * (ri - 1), own),
            block(ro * (ri - 1), own),
            block(ro - 1, own),
            block(ro - 1, own),
            block(nrow, rows1),
            block(nrow - 1, rows1),
            block(ncol, rows2),
            block(ncol - 1, rows2),
            pltpu.VMEM((nrow, ncol, rows2, width), BF16),
            dma((5,)),
            dma((ag_sends(ro, ri),)),
            dma((nrow,)),
            dma((2, max(halves * co * (ci - 1), 1))),
            dma((2, max(halves * (co - 1), 1))),
            dma((halves * ag_sends(co, ci),)),
            dma((halves * ncol,)),
            dma((2, max(ro * (ri - 1), 1))),
            dma((2, max(ro - 1, 1))),
            dma((2, nrow)),
            dma((2, ncol)),
            dma((ncol,)),
            dma((ncol,)),
            dma((nrow,)),
            dma((nrow,)),
        ]
        anyspace = pl.BlockSpec(memory_space=pl.ANY)
        vmem = pl.BlockSpec(memory_space=pltpu.VMEM)
        shapes = (
            jax.ShapeDtypeStruct((own, width), BF16),
            jax.ShapeDtypeStruct((own, width), BF16),
            jax.ShapeDtypeStruct((width, width), F32),
        )
        outs = pl.pallas_call(
            functools.partial(kernel, dims),
            out_shape=shapes,
            in_specs=[pl.BlockSpec(memory_space=pltpu.SMEM), vmem] + [anyspace] * 4,
            out_specs=[vmem] * 3,
            scratch_shapes=scratch,
            compiler_params=pltpu.CompilerParams(
                collective_id=0,
                has_side_effects=True,
                vmem_limit_bytes=66 * 1000 * 1000,
            ),
        )(block_count, block_pos, features, weight, grad_out, adj_values)
        return pl.pallas_call(
            hand_on, out_shape=shapes, in_specs=[vmem] * 3, out_specs=[vmem] * 3
        )(*outs)

    placed = (
        P(("col", "row"), None),
        P(),
        P(("row", "col"), None),
        P("row", "col", None),
        P("row", "col"),
        P("row", "col"),
    )
    return jax.shard_map(
        body,
        mesh=mesh,
        in_specs=placed,
        out_specs=(P(("row", "col"), None), P(("col", "row"), None), P()),
        check_vma=False,
    )
```

time: 353 us -> 59.5 us (0.17)
  waiting for transfers between devices: 255 us -> 0 us
  Pallas kernels: 0 us -> 58.1 us
  matrix products: 47.9 us -> 0 us
  local copies, waits for them, and re-layouts: 19.8 us -> 0 us
  between operations: 14.5 us -> 1.29 us
  blocking collectives: 8.65 us -> 0 us
  other arithmetic: 4.97 us -> 0 us
    psum x1 -> x0, waiting for transfers between devices: 129 us -> none  [body(): grad_weight = lax.psum(local_weight, ('row', 'col'))]
    reduce_scatter x2 -> x0, waiting for transfers between devices: 85.5 us -> none  [the longest x1 65.1 us: body(): lax.psum_scatter(partial_value.astype(jnp.bfloat16), 'col', scatter_dimen...]
    pallas_call x0 -> x2, Pallas kernels: none -> 58.1 us  [the longest x1 56.2 us: body(): pl.pallas_call(functools.partial(kernel, dims), out_shape=shapes, in_spec...]
    dot_general x27 -> x0, matrix products: 47.9 us -> none  [the longest x6 20.7 us: step(): return (totals + jnp.einsum('bk,kif->bif', onehot, prod), None)]
    all_gather x1 -> x0, waiting for transfers between devices: 40.2 us -> none  [body(): grad_panel = lax.all_gather(grad_hidden, 'col', axis=0, tiled=True)]
    gather x12 -> x0, local copies, waits for them, and re-layouts: 14.7 us -> none  [the longest x6 11 us: step(): picked = blocks[rows_idx]]
    all_gather x1 -> x0, blocking collectives: 8.65 us -> none  [body(): panel = lax.all_gather(projected, 'row', axis=0, tiled=True)]
  transfers between devices with their start and end apart: 4 -> 0, of which waited for: 4 -> 0; matrix products, arithmetic and copies ran while one was open for 1% -> 0% of each run, Pallas kernels for 0% -> 0%
where the time goes in v2:
time: 59.5 us; the launch traced here: 59.4 us
  Pallas kernels  58.1 us (98%)
  between operations  1.29 us (2%)
    pallas_call x1, Pallas kernels, body(): pl.pallas_call(functools.partial(kernel, dims), out_shape=shapes, in_spec...  56.2 us
    pallas_call x1, Pallas kernels, body(): pl.pallas_call(hand_on, out_shape=shapes, in_specs=[vmem] * 3, out_specs=...  1.88 us

profile of v2, /device:TPU:0, one launch (start us, length us, event | category | flops | bytes accessed | tf_op | source)
XLA Modules:
  0.0 59.4 jit_solution(791991601110423736)
XLA Ops:
  1.3 56.2 %shard_map.85 = (bf16[256,256]{1,0:T(8,128)(2,1)}, bf16[256,256]{1,0:T(8,128)(2,1)}, f32[256,256]{1,0:T(8,128)}) custom-call(s32[1,1]{1,0:T(1,128)S(6)} %copy.9.count_ref, s32[1,96]{1,0:T(1,128)} %pos_ref.1, bf16[256,256]{1,0:T(8,128)(2,1)} %feat_ref.1, bf16[256,256]{1,0:T(8,128)(2,1)} %weight_ref.1, bf16[256,256]{1,0:T(8,128)(2,1)} %gout_ref.1, ...), custom_call_target="tpu_custom_call" | custom-call | tf_op jit(solution)/shard_map/pallas_call | solution.py:504
  57.5 1.9 %shard_map.86 = (bf16[256,256]{1,0:T(8,128)(2,1)}, bf16[256,256]{1,0:T(8,128)(2,1)}, f32[256,256]{1,0:T(8,128)}) custom-call(bf16[256,256]{1,0:T(8,128)(2,1)} %get-tuple-element.6.a_in, bf16[256,256]{1,0:T(8,128)(2,1)} %get-tuple-element.7.b_in, f32[256,256]{1,0:T(8,128)} %get-tuple-element.8.c_in), custom_call_target="tpu_custom_call" | custom-call | tf_op jit(solution)/shard_map/pallas_call | solution.py:516

commit v3 on v2

--- a/solution.py
+++ b/solution.py
@@ -24,7 +24,7 @@
         self.outer, self.inner, self.n_out, self.n_in = outer, inner, n_out, n_in
         self.s_in, self.r_in, self.s_out, self.r_out = bufs
         self.sem_in, self.sem_out = sems
-        self.sent, self.totals = [], {}
+        self.sent, self.totals, self.held, self.line = [], {}, {}, None
 
     def to(self, d):
         return lax.rem(self.outer + d, self.n_out)
@@ -99,14 +99,14 @@
         self.outer, self.inner, self.n_out, self.n_in = outer, inner, n_out, n_in
         self.buf, self.send, self.recv = buf, send, recv
         self.me = outer * n_in + inner
-        self.sent = []
+        self.sent, self.maybe, self.slots, self.line = [], [], 0, None
 
     def push(self, block, h, peer):
         at = block * self.halves + h
         copy = self.link(
             self.buf.at[at],
             self.buf.at[at],
-            self.send.at[len(self.sent)],
+            self.send.at[len(self.sent) + self.slots],
             self.recv.at[at],
             self.axis,
             peer,
@@ -141,6 +141,139 @@
             block = lax.rem(self.outer + d, self.n_out) * self.n_in + lax.rem(
                 self.inner + e, self.n_in
             )
+            self.arrive(block, h)
+            blocks.append(block)
+        return blocks
+
+
+class Line:
+    def __init__(self, at):
+        self.central = lax.rem(lax.div(at + 1, 2), 2) == 1
+        self.mate = at + 1 - 2 * lax.rem(at, 2)
+        self.near = 2 - lax.div(at, 2)
+        self.place = (at, self.mate, self.near, 3 * (self.near - 1))
+
+
+class TreeReduce(Reduce):
+    def to(self, d):
+        return self.line.place[d]
+
+    def hop(self, h, d, peer, landing):
+        slot = h * 4 + d
+        copy = self.link(
+            self.s_out.at[slot],
+            self.r_out.at[h * 4 + landing],
+            self.sem_out.at[0, slot],
+            self.sem_out.at[1, h * 4 + landing],
+            self.axis,
+            peer * self.n_in + self.inner,
+        )
+        copy.start()
+        self.sent.append(copy)
+
+    def landed(self, h, slot):
+        at = h * 4 + slot
+        self.link(
+            self.r_out.at[at],
+            self.r_out.at[at],
+            self.sem_out.at[0, at],
+            self.sem_out.at[1, at],
+            self.axis,
+            0,
+        ).wait_recv()
+        return self.r_out[at].astype(F32)
+
+    def middle(self, h, d):
+        value = self.part(self.to(d) * self.n_in + self.inner, h)
+        for e in range(1, self.n_in):
+            at = (h * self.n_out + self.to(d)) * (self.n_in - 1) + e - 1
+            self.link(
+                self.r_in.at[at],
+                self.r_in.at[at],
+                self.sem_in.at[0, 0],
+                self.sem_in.at[1, at],
+                self.axis,
+                0,
+            ).wait_recv()
+            value = value + self.r_in[at].astype(F32)
+        line = self.line
+        if d == 0:
+            self.totals[h] = value
+        elif d == 1:
+            self.s_out[h * 4 + d] = value.astype(BF16)
+            self.hop(h, d, line.mate, 0)
+        else:
+            self.s_out[h * 4 + d] = value.astype(BF16)
+            rim = jnp.logical_not(line.central)
+
+            @pl.when(rim)
+            def _():
+                self.hop(h, d, line.mate, d)
+
+            self.sent.pop()
+            self.held[h, d] = value
+
+    def join(self, h, d):
+        line = self.line
+
+        @pl.when(line.central)
+        def _():
+            total = self.held[h, d] + self.landed(h, d)
+            self.s_out[h * 4 + d] = total.astype(BF16)
+            self.hop(h, d, line.place[d], 1)
+
+        self.sent.pop()
+        slot = h * 4 + d
+        self.sent.append(
+            self.link(
+                self.s_out.at[slot],
+                self.s_out.at[slot],
+                self.sem_out.at[0, slot],
+                self.sem_out.at[1, slot],
+                self.axis,
+                0,
+            )
+        )
+
+    def end(self, h):
+        return self.totals[h] + self.landed(h, 0) + self.landed(h, 1)
+
+
+class TreeGather(Gather):
+    def start(self, h):
+        self.push(self.me, h, self.line.near * self.n_in + self.inner)
+        self.push(self.me, h, self.line.mate * self.n_in + self.inner)
+        self.forward(self.me, h)
+
+    def from_outer(self, h, d):
+        block = self.line.place[d] * self.n_in + self.inner
+        self.arrive(block, h)
+        if d > 1:
+
+            @pl.when(self.line.central)
+            def _():
+                self.push(block, h, self.line.mate * self.n_in + self.inner)
+
+            self.sent.pop()
+            at = self.me * self.halves + h
+            self.maybe.append(
+                self.link(
+                    self.buf.at[at],
+                    self.buf.at[at],
+                    self.send.at[len(self.sent) + self.slots],
+                    self.recv.at[at],
+                    self.axis,
+                    0,
+                )
+            )
+            self.slots += 1
+        self.forward(block, h)
+        return [block]
+
+    def from_inner(self, h, d):
+        blocks = []
+        for e in range(1, self.n_in):
+            block = self.line.place[d] * self.n_in + lax.rem(self.inner + e, self.n_in)
             self.arrive(block, h)
             blocks.append(block)
         return blocks
@@ -277,11 +410,13 @@
             preferred_element_type=F32,
         )
 
-    rsc = Reduce(
+    line = Line(cz)
+    rsc = TreeReduce(
         remote, "col", cz, cy, co, ci, forward, (cs_y, cr_y, cs_z, cr_z), (sem_cy, sem_cz)
     )
-    agc = Gather(remote, "col", cz, cy, co, ci, halves, ghs, sem_g, sem_gr)
-    order = list(range(1, co)) + [0]
+    agc = TreeGather(remote, "col", cz, cy, co, ci, halves, ghs, sem_g, sem_gr)
+    rsc.line = agc.line = line
+    order = [2, 3, 1, 0]
     for h in range(halves):
         for d in order:
             rsc.start(h, d)
@@ -300,12 +435,13 @@
         agc.start(h)
         act_ref[at, :] = (hidden * sigma).astype(BF16)
 
-    for d in order:
-        rsc.middle(0, d)
-    for h in range(1, halves):
+    for h in range(halves):
         for d in order[:-1]:
             rsc.middle(h, d)
-        owner(h - 1)
+        if h:
+            owner(h - 1)
+        rsc.join(h, 2)
+        rsc.join(h, 3)
         rsc.middle(h, 0)
     owner(halves - 1)
 
@@ -418,6 +554,11 @@
     gin_ref[...] = lax.dot_general(
         rsr.end(0).astype(BF16), wbuf[...], (((1,), (1,)), ((), ())), preferred_element_type=F32
     ).astype(BF16)
+    @pl.when(line.central)
+    def _():
+        for copy in agc.maybe:
+            copy.wait_send()
+
     for copy in g1.sent + rsc.sent + agc.sent + rsr.sent + w1 + w2 + w3 + w4c:
         copy.wait_send()
 
@@ -431,7 +572,7 @@
 def solution(mesh):
     nrow, ncol = mesh.shape["row"], mesh.shape["col"]
     ro, ri = split_axis(nrow, 2)
-    co = 4 if ncol % 4 == 0 else 1
+    co = 4
     ci = ncol // co
     halves = 2
     dims = (nrow, ncol, ro, ri, co, ci, halves)
@@ -464,8 +605,8 @@
             pltpu.VMEM((own, width), BF16),
             block(halves * co * (ci - 1), half),
             block(halves * co * (ci - 1), half),
-            block(halves * (co - 1), half),
-            block(halves * (co - 1), half),
+            block(halves * co, half),
+            block(halves * co, half),
             pltpu.VMEM((own, width), BF16),
             block(ncol * halves, half),
             pltpu.VMEM((cols_tile, width), F32),
@@ -482,8 +623,8 @@
             dma((ag_sends(ro, ri),)),
             dma((nrow,)),
             dma((2, max(halves * co * (ci - 1), 1))),
-            dma((2, max(halves * (co - 1), 1))),
-            dma((halves * ag_sends(co, ci),)),
+            dma((2, halves * co)),
+            dma((halves * (ag_sends(co, ci) + 1),)),
             dma((halves * ncol,)),
             dma((2, max(ro * (ri - 1), 1))),
             dma((2, max(ro - 1, 1))),

time: 59.5 us -> 56.6 us (0.951)
  Pallas kernels: 58.1 us -> 55.1 us
    pallas_call x1, Pallas kernels: 56.2 us -> 53.2 us  [body(): pl.pallas_call(functools.partial(kernel, dims), out_shape=shapes, in_spec...]
where the time goes in v3:
time: 56.6 us; the launch traced here: 56.4 us
  Pallas kernels  55.1 us (97%)
  between operations  1.29 us (2%)
    pallas_call x1, Pallas kernels, body(): pl.pallas_call(functools.partial(kernel, dims), out_shape=shapes, in_spec...  53.2 us
    pallas_call x1, Pallas kernels, body(): pl.pallas_call(hand_on, out_shape=shapes, in_specs=[vmem] * 3, out_specs=...  1.88 us

profile of v3, /device:TPU:0, one launch (start us, length us, event | category | flops | bytes accessed | tf_op | source)
XLA Modules:
  0.0 56.4 jit_solution(8530304809150854353)
XLA Ops:
  1.3 53.2 %shard_map.85 = (bf16[256,256]{1,0:T(8,128)(2,1)}, bf16[256,256]{1,0:T(8,128)(2,1)}, f32[256,256]{1,0:T(8,128)}) custom-call(s32[1,1]{1,0:T(1,128)S(6)} %copy.9.count_ref, s32[1,96]{1,0:T(1,128)} %pos_ref.1, bf16[256,256]{1,0:T(8,128)(2,1)} %feat_ref.1, bf16[256,256]{1,0:T(8,128)(2,1)} %weight_ref.1, bf16[256,256]{1,0:T(8,128)(2,1)} %gout_ref.1, ...), custom_call_target="tpu_custom_call" | custom-call | tf_op jit(solution)/shard_map/pallas_call | solution.py:645
  54.5 1.9 %shard_map.86 = (bf16[256,256]{1,0:T(8,128)(2,1)}, bf16[256,256]{1,0:T(8,128)(2,1)}, f32[256,256]{1,0:T(8,128)}) custom-call(bf16[256,256]{1,0:T(8,128)(2,1)} %get-tuple-element.6.a_in, bf16[256,256]{1,0:T(8,128)(2,1)} %get-tuple-element.7.b_in, f32[256,256]{1,0:T(8,128)} %get-tuple-element.8.c_in), custom_call_target="tpu_custom_call" | custom-call | tf_op jit(solution)/shard_map/pallas_call | solution.py:657

commit v4 on v3

--- a/solution.py
+++ b/solution.py
@@ -495,11 +495,12 @@
         copy.start()
         w2.append(copy)
 
+    arrived = []
     for d in range(1, co):
-        backward(agc.from_outer(last, d))
-    for h in range(last):
-        for d in range(co):
-            agc.from_inner(h, d)
+        arrived += agc.from_outer(last, d)
+        if d > 1:
+            backward([arrived.pop(0)])
+    backward(arrived)
 
     share = ws2[col].astype(F32)
     for d, copy in enumerate(w2):
@@ -516,17 +517,20 @@
         w3.append(copy)
 
     for d in range(co):
+        for h in range(last):
+            agc.from_inner(h, d)
         backward(agc.from_inner(last, d))
 
     def back(block, h):
-        return acc[rows(block), :]
+        return acc[rows(block, h, half), :]
 
     rsr = Reduce(
         remote, "row", rx, rc, ro, ri, back, (rs_y, rr_y, rs_z, rr_z), (sem_ry, sem_rz)
     )
     order = list(range(1, ro)) + [0]
-    for d in order:
-        rsr.start(0, d)
+    for h in range(halves):
+        for d in order:
+            rsr.start(h, d)
 
     for d in range(1, ncol):
         source = lax.rem(col + d, ncol)
@@ -540,8 +544,9 @@
         copy.start()
         w4c.append(copy)
 
-    for d in order:
-        rsr.middle(0, d)
+    for h in range(halves):
+        for d in order:
+            rsr.middle(h, d)
     for d in range(1, nrow):
         source = lax.rem(row + d, nrow)
         remote(
@@ -551,9 +556,10 @@
         for k in range(ncol):
             at = r * rows1 + k * rows2
             gw_ref[at : at + rows2, :] = w4[r, k].astype(F32)
-    gin_ref[...] = lax.dot_general(
-        rsr.end(0).astype(BF16), wbuf[...], (((1,), (1,)), ((), ())), preferred_element_type=F32
-    ).astype(BF16)
+    for h in range(halves):
+        gin_ref[h * half : (h + 1) * half, :] = lax.dot_general(
+            rsr.end(h).astype(BF16), wbuf[...], (((1,), (1,)), ((), ())), preferred_element_type=F32
+        ).astype(BF16)
     @pl.when(line.central)
     def _():
         for copy in agc.maybe:
@@ -610,10 +616,10 @@
             pltpu.VMEM((own, width), BF16),
             block(ncol * halves, half),
             pltpu.VMEM((cols_tile, width), F32),
-            block(ro * (ri - 1), own),
-            block(ro * (ri - 1), own),
-            block(ro - 1, own),
-            block(ro - 1, own),
+            block(halves * ro * (ri - 1), half),
+            block(halves * ro * (ri - 1), half),
+            block(halves * (ro - 1), half),
+            block(halves * (ro - 1), half),
             block(nrow, rows1),
             block(nrow - 1, rows1),
             block(ncol, rows2),
@@ -626,8 +632,8 @@
             dma((2, halves * co)),
             dma((halves * (ag_sends(co, ci) + 1),)),
             dma((halves * ncol,)),
-            dma((2, max(ro * (ri - 1), 1))),
-            dma((2, max(ro - 1, 1))),
+            dma((2, max(halves * ro * (ri - 1), 1))),
+            dma((2, max(halves * (ro - 1), 1))),
             dma((2, nrow)),
             dma((2, ncol)),
             dma((ncol,)),

time: 56.6 us -> 56.2 us (level)
  no operation moved by 1% of the time
where the time goes in v4:
time: 56.2 us; the launch traced here: 56.1 us
  Pallas kernels  54.8 us (98%)
  between operations  1.29 us (2%)
    pallas_call x1, Pallas kernels, body(): pl.pallas_call(functools.partial(kernel, dims), out_shape=shapes, in_spec...  52.9 us
    pallas_call x1, Pallas kernels, body(): pl.pallas_call(hand_on, out_shape=shapes, in_specs=[vmem] * 3, out_specs=...  1.88 us

profile of v4, /device:TPU:0, one launch (start us, length us, event | category | flops | bytes accessed | tf_op | source)
XLA Modules:
  0.0 56.1 jit_solution(13224246349165826145)
XLA Ops:
  1.3 52.9 %shard_map.85 = (bf16[256,256]{1,0:T(8,128)(2,1)}, bf16[256,256]{1,0:T(8,128)(2,1)}, f32[256,256]{1,0:T(8,128)}) custom-call(s32[1,1]{1,0:T(1,128)S(6)} %copy.9.count_ref, s32[1,96]{1,0:T(1,128)} %pos_ref.1, bf16[256,256]{1,0:T(8,128)(2,1)} %feat_ref.1, bf16[256,256]{1,0:T(8,128)(2,1)} %weight_ref.1, bf16[256,256]{1,0:T(8,128)(2,1)} %gout_ref.1, ...), custom_call_target="tpu_custom_call" | custom-call | tf_op jit(solution)/shard_map/pallas_call | solution.py:651
  54.2 1.9 %shard_map.86 = (bf16[256,256]{1,0:T(8,128)(2,1)}, bf16[256,256]{1,0:T(8,128)(2,1)}, f32[256,256]{1,0:T(8,128)}) custom-call(bf16[256,256]{1,0:T(8,128)(2,1)} %get-tuple-element.6.a_in, bf16[256,256]{1,0:T(8,128)(2,1)} %get-tuple-element.7.b_in, f32[256,256]{1,0:T(8,128)} %get-tuple-element.8.c_in), custom_call_target="tpu_custom_call" | custom-call | tf_op jit(solution)/shard_map/pallas_call | solution.py:663
